TPU v7x, 32 devices: a whole 2x2x4 slice. The times are simulated.
32 devices in a mesh: dp: 4 (over y, x), space: 8 (over z, core).
Axes of the slice: x: 2, y: 2, z: 4, core: 2. Of those that a mesh axis runs over, the one named last changes fastest.
Arguments:
- features: bfloat16 [4, 2048, 256], P('dp', 'space'), may hold values from -6 to 6
- neighbours: int32 [4, 27, 2048], P('dp', None, 'space'), may hold values from -1 to 2047, as said below
- parents: int32 [4, 2048], P('dp', 'space'), may hold values from 0 to 511, as said below
- conv_first: bfloat16 [27, 256, 256], replicated, may hold values from -0.078125 to 0.078125
- conv_second: bfloat16 [27, 256, 256], replicated, may hold values from -0.078125 to 0.078125
- gain_first: float32 [256], replicated, may hold values from 0.1 to 1.9
- gain_second: float32 [256], replicated, may hold values from 0.1 to 1.9
- down_weight: bfloat16 [256, 512], replicated, may hold values from -0.375 to 0.375
- cotangent: bfloat16 [4, 512, 512], P('dp', 'space'), may hold values from -6 to 6
Outputs:
- fine_out: bfloat16 [4, 2048, 256], P('dp', 'space')
- coarse: bfloat16 [4, 512, 512], P('dp', 'space')
- down_grad: float32 [256, 512], replicated
Inputs may be any that keep to these rules, and one draw needn't show every extreme that they name: `neighbours`: for a site s of the block [d * 256, (d + 1) * 256), every entry is -1 or lies in [(d - 1) * 256, (d + 2) * 256); entry 13 is s itself. The parents of the sites of the block [d * 256, (d + 1) * 256) never decrease along the block and lie in [d * 64, (d + 2) * 64).
All inputs are finite; a program needn't handle non-finite values.
Results may differ from a plain program's by a relative error of at most 0.0057.
Values may be sent and summed in bfloat16 or wider, within the bound.
A program may use at most 64 MiB of HBM per device.

v0:
```python
import math
import jax
import jax.numpy as jnp
from jax import lax
from jax.sharding import PartitionSpec as P


def extended(cells, sides, width):
    for axis, dim in sides:
        count = lax.axis_size(axis)
        ends = count - 1
        head = lax.slice_in_dim(cells, 0, width, axis=dim)
        tail = lax.slice_in_dim(cells, cells.shape[dim] - width, cells.shape[dim], axis=dim)
        cells = jnp.concatenate(
            [
                lax.ppermute(tail, axis, [(i, (i + 1) % count) for i in range(ends)]),
                cells,
                lax.ppermute(head, axis, [((i + 1) % count, i) for i in range(ends)]),
            ],
            axis=dim,
        )
    return cells


def from_behind(array, axis, by):
    length = lax.axis_size(axis)
    pairs = [(i, i + by) for i in range(length) if 0 <= i + by < length]
    return lax.ppermute(array, axis, pairs)


def convolve(field, tap_lists, weights):
    site_rows = field.shape[1]
    nearby = extended(field, (("space", 1),), site_rows)
    lowest = (lax.axis_index("space") - 1) * site_rows
    lookup = jnp.where(tap_lists < 0, 3 * site_rows, tap_lists - lowest)
    window_ids = jnp.arange(3 * site_rows, dtype=jnp.int32)

    def one_tap(running, inputs):
        rows_now, weight = inputs
        selector = (rows_now[:, :, None] == window_ids[None, None, :]).astype(jnp.bfloat16)
        picked = jnp.einsum(
            "wsr,wrc->wsc", selector, nearby, preferred_element_type=jnp.float32
        ).astype(jnp.bfloat16)
        return (
            running + jnp.einsum("wsc,cd->wsd", picked, weight, preferred_element_type=jnp.float32),
            None,
        )

    start = jnp.zeros((field.shape[0], site_rows, weights.shape[2]), jnp.float32)
    running, _ = lax.scan(one_tap, start, (jnp.moveaxis(lookup, 1, 0), weights))
    return running


def settle(running, gain):
    inverse = lax.rsqrt(jnp.mean(running * running, axis=-1, keepdims=True) + 1e-05)
    return jax.nn.silu(running * inverse * gain)


def body(
    features,
    neighbours,
    parents,
    conv_first,
    conv_second,
    gain_first,
    gain_second,
    down_weight,
    cotangent,
):
    middle = settle(convolve(features, neighbours, conv_first), gain_first).astype(jnp.bfloat16)
    fine_out = (
        features.astype(jnp.float32)
        + settle(convolve(middle, neighbours, conv_second), gain_second)
    ).astype(jnp.bfloat16)
    par_rows = cotangent.shape[1]
    owner_id = lax.axis_index("space")
    world_rows = features.shape[0]
    parent_ids = owner_id * par_rows + jnp.arange(2 * par_rows, dtype=jnp.int32)
    onehot = (parents[:, None, :] == parent_ids[None, :, None]).astype(jnp.bfloat16)
    partial_value = jnp.einsum("wps,wsc->wpc", onehot, fine_out, preferred_element_type=jnp.float32)
    tallies = jnp.sum(onehot.astype(jnp.float32), axis=2)
    moved = from_behind((partial_value[:, par_rows:], tallies[:, par_rows:]), "space", 1)
    parent_sums = partial_value[:, :par_rows] + moved[0]
    counts = tallies[:, :par_rows] + moved[1]
    pooled = (parent_sums / jnp.maximum(counts, 1.0)[:, :, None]).astype(jnp.bfloat16)
    coarse = jnp.einsum(
        "wpc,cd->wpd", pooled, down_weight, preferred_element_type=jnp.float32
    ).astype(jnp.bfloat16)
    local_grad = jnp.einsum("wpc,wpd->cd", pooled, cotangent, preferred_element_type=jnp.float32)
    worlds_all = world_rows * lax.axis_size("dp")
    parents_all = par_rows * lax.axis_size("space")
    down_grad = lax.psum(local_grad, ("dp", "space")) * (1.0 / math.sqrt(worlds_all * parents_all))
    return (fine_out, coarse, down_grad)


def solution(mesh):
    return jax.shard_map(
        body,
        mesh=mesh,
        in_specs=(
            P("dp", "space", None),
            P("dp", None, "space"),
            P("dp", "space"),
            P(),
            P(),
            P(),
            P(),
            P(),
            P("dp", "space", None),
        ),
        out_specs=(P("dp", "space", None), P("dp", "space", None), P()),
        check_vma=False,
    )
```

profile of v0, /device:TPU:0, one launch (start us, length us, event | category | flops | bytes accessed | tf_op | source)
XLA Modules:
  0.0 252.0 jit_solution(10413457237684646482)
XLA Ops:
  7.2 2.5 %collective-permute-start = (bf16[1,256,256]{2,1,0:T(8,128)(2,1)}, bf16[1,256,256]{2,1,0:T(8,128)(2,1)S(1)}, u32[]{:S(2)}, u32[]{:S(2)}) collective-permute-start(bf16[1,256,256]{2,1,0:T(8,128)(2,1)} %param.13), channel_id=1, source_target_pairs={{0,1},{1,2},{2,3},{3,4},{4,5},{5,6},{6,7},{8,9},{9,10},{10,11},{11... | collective-permute-start | bytes 393224 | tf_op jit(solution)/shard_map/ppermute | solution.py:16
  9.8 1.3 collective-permute-start.1
  11.9 3.5 %collective-permute-done.1 = bf16[1,256,256]{2,1,0:T(8,128)(2,1)S(1)} collective-permute-done((bf16[1,256,256]{2,1,0:T(8,128)(2,1)}, bf16[1,256,256]{2,1,0:T(8,128)(2,1)S(1)}, u32[]{:S(2)}, u32[]{:S(2)}) %collective-permute-start.1) | collective-permute-done | bytes 131104 | tf_op jit(solution)/shard_map/ppermute | solution.py:18
  16.4 39.3 %while.22 = (s32[]{:T(128)}, f32[1,256,256]{2,1,0:T(8,128)S(1)}, s32[27,1,256]{2,1,0:T(1,128)S(1)}, bf16[1,768,256]{2,1,0:T(8,128)(2,1)S(1)}, bf16[27,256,256]{2,1,0:T(8,128)(2,1)}, /*index=5*/s32[]{:T(128)}, s32[]{:T(128)}) while((s32[]{:T(128)}, f32[1,256,256]{2,1,0:T(8,128)S(1)}, s32[27,1,256]{2,1,0:T(1,128)S(1)}, ...), condition=%wide.region_1.2_spmd.clone, body=%wide.region_0.1_spmd.clone.sunk | while | flops 134610944 | bytes 1052251 | solution.py:50
  16.4 1.4 fusion.50
  17.8 1.4 fusion.50
  19.3 1.4 fusion.50
  20.8 1.4 fusion.50
  22.2 1.4 fusion.50
  23.7 1.4 fusion.50
  25.1 1.4 fusion.50
  26.6 1.4 fusion.50
  28.0 1.4 fusion.50
  29.5 1.4 fusion.50
  31.0 1.4 fusion.50
  32.4 1.4 fusion.50
  33.9 1.4 fusion.50
  35.3 1.4 fusion.50
  36.8 1.4 fusion.50
  38.2 1.4 fusion.50
  39.7 1.4 fusion.50
  41.2 1.4 fusion.50
  42.6 1.4 fusion.50
  44.1 1.4 fusion.50
  45.5 1.4 fusion.50
  47.0 1.4 fusion.50
  48.4 1.4 fusion.50
  49.9 1.4 fusion.50
  51.3 1.4 fusion.50
  52.8 1.4 fusion.50
  54.3 1.4 fusion.50
  56.0 5.5 %collective-permute-start.2 = (bf16[1,256,256]{2,1,0:T(8,128)(2,1)S(1)}, bf16[1,256,256]{2,1,0:T(8,128)(2,1)S(1)}, u32[]{:S(2)}, u32[]{:S(2)}) collective-permute-start(bf16[1,256,256]{2,1,0:T(8,128)(2,1)S(1)} %multiply_convert_fusion), channel_id=1, source_target_pairs={{0,1},{1,2},{2,3},{3,4},{4,5},{5,6},{6,7},{8,9},{9,10},{10,11},{11... | collective-permute-start | bytes 393224 | tf_op jit(solution)/shard_map/ppermute | solution.py:16
  63.0 3.0 %collective-permute-start.5 = (f32[1,64]{1,0:T(1,128)S(1)}, f32[1,64]{1,0:T(1,128)S(1)}, u32[]{:S(2)}, u32[]{:S(2)}) collective-permute-start(f32[1,64]{1,0:T(1,128)S(1)} %slice.15), channel_id=1, source_target_pairs={{0,1},{1,2},{2,3},{3,4},{4,5},{5,6},{6,7},{8,9},{9,10},{10,11},{11... | collective-permute-start | bytes 776 | tf_op jit(solution)/shard_map/ppermute | solution.py:28
  66.2 39.3 %while.23 = (s32[]{:T(128)}, f32[1,256,256]{2,1,0:T(8,128)S(1)}, s32[27,1,256]{2,1,0:T(1,128)S(1)}, bf16[1,768,256]{2,1,0:T(8,128)(2,1)S(1)}, bf16[27,256,256]{2,1,0:T(8,128)(2,1)}, /*index=5*/s32[]{:T(128)}, s32[]{:T(128)}) while((s32[]{:T(128)}, f32[1,256,256]{2,1,0:T(8,128)S(1)}, s32[27,1,256]{2,1,0:T(1,128)S(1)}, ...), condition=%wide.region_4.5_spmd.clone, body=%wide.region_3.4_spmd.clone.sunk | while | flops 134610944 | bytes 1052251 | solution.py:50
  66.2 1.4 fusion.54
  67.7 1.4 fusion.54
  69.1 1.4 fusion.54
  70.6 1.4 fusion.54
  72.0 1.4 fusion.54
  73.5 1.4 fusion.54
  74.9 1.4 fusion.54
  76.4 1.4 fusion.54
  77.9 1.4 fusion.54
  79.3 1.4 fusion.54
  80.8 1.4 fusion.54
  82.2 1.4 fusion.54
  83.7 1.4 fusion.54
  85.1 1.4 fusion.54
  86.6 1.4 fusion.54
  88.1 1.4 fusion.54
  89.5 1.4 fusion.54
  91.0 1.4 fusion.54
  92.4 1.4 fusion.54
  93.9 1.4 fusion.54
  95.3 1.4 fusion.54
  96.8 1.4 fusion.54
  98.3 1.4 fusion.54
  99.7 1.4 fusion.54
  101.2 1.4 fusion.54
  102.6 1.4 fusion.54
  104.1 1.4 fusion.54
  106.1 3.6 %collective-permute-start.4 = (f32[1,64,256]{2,1,0:T(8,128)S(1)}, f32[1,64,256]{2,1,0:T(8,128)S(1)}, u32[]{:S(2)}, u32[]{:S(2)}) collective-permute-start(f32[1,64,256]{2,1,0:T(8,128)S(1)} %slice.17), channel_id=1, source_target_pairs={{0,1},{1,2},{2,3},{3,4},{4,5},{5,6},{6,7},{8,9},{9,10},{10,11},{11... | collective-permute-start | bytes 196616 | tf_op jit(solution)/shard_map/ppermute | solution.py:28
  112.5 130.8 %all-reduce.2.cloned.1.call-done = f32[256,512]{1,0:T(8,128)} async-done(((f32[256,512]{1,0:T(8,128)}), f32[256,512]{1,0:T(8,128)}) %all-reduce.2.cloned.1.call-update) | async-done | bytes 524304 | tf_op jit(solution)/shard_map/psum | solution.py:92
  243.2 1.9 broadcast_multiply_fusion
  (96 shorter events, 7.3 us)
Async XLA Ops:
  7.2 104.5 %copy-start = (bf16[256,512]{1,0:T(8,128)(2,1)S(1)}, bf16[256,512]{1,0:T(8,128)(2,1)}, u32[]{:S(2)}) copy-start(bf16[256,512]{1,0:T(8,128)(2,1)} %param.20) | copy-start | bytes 786436
  7.2 48.7 %copy-start.5 = (f32[256]{0:T(256)S(1)}, f32[256]{0:T(256)}, u32[]{:S(2)}) copy-start(f32[256]{0:T(256)} %param.18) | copy-start | bytes 3076
  7.2 55.6 %copy-start.4 = (s32[1,256]{1,0:T(1,128)S(1)}, s32[1,256]{1,0:T(1,128)}, u32[]{:S(2)}) copy-start(s32[1,256]{1,0:T(1,128)} %param.15) | copy-start | bytes 3076
  7.2 236.0 %all-reduce.2.cloned.1.call-start = ((), (), s32[]{:S(2)}) async-start(), calls=%async_computation | async-start | bytes 1048576 | tf_op jit(solution)/shard_map/psum | solution.py:92
  7.2 4.6 %collective-permute-start = (bf16[1,256,256]{2,1,0:T(8,128)(2,1)}, bf16[1,256,256]{2,1,0:T(8,128)(2,1)S(1)}, u32[]{:S(2)}, u32[]{:S(2)}) collective-permute-start(bf16[1,256,256]{2,1,0:T(8,128)(2,1)} %param.13), channel_id=1, source_target_pairs={{0,1},{1,2},{2,3},{3,4},{4,5},{5,6},{6,7},{8,9},{9,10},{10,11},{11... | collective-permute-start | bytes 393224 | tf_op jit(solution)/shard_map/ppermute | solution.py:16
  9.8 5.6 %collective-permute-start.1 = (bf16[1,256,256]{2,1,0:T(8,128)(2,1)}, bf16[1,256,256]{2,1,0:T(8,128)(2,1)S(1)}, u32[]{:S(2)}, u32[]{:S(2)}) collective-permute-start(bf16[1,256,256]{2,1,0:T(8,128)(2,1)} %param.13), channel_id=1, source_target_pairs={{1,0},{2,1},{3,2},{4,3},{5,4},{6,5},{7,6},{9,8},{10,9},{11,10},{12... | collective-permute-start | bytes 393224 | tf_op jit(solution)/shard_map/ppermute | solution.py:18
  55.7 50.0 %copy-start.2 = (bf16[1,256,256]{2,1,0:T(8,128)(2,1)S(1)}, bf16[1,256,256]{2,1,0:T(8,128)(2,1)}, u32[]{:S(2)}) copy-start(bf16[1,256,256]{2,1,0:T(8,128)(2,1)} %param.13) | copy-start | bytes 393220
  55.7 49.9 %copy-start.6 = (f32[256]{0:T(256)S(1)}, f32[256]{0:T(256)}, u32[]{:S(2)}) copy-start(f32[256]{0:T(256)} %param.19) | copy-start | bytes 3076
  56.0 10.1 %collective-permute-start.2 = (bf16[1,256,256]{2,1,0:T(8,128)(2,1)S(1)}, bf16[1,256,256]{2,1,0:T(8,128)(2,1)S(1)}, u32[]{:S(2)}, u32[]{:S(2)}) collective-permute-start(bf16[1,256,256]{2,1,0:T(8,128)(2,1)S(1)} %multiply_convert_fusion), channel_id=1, source_target_pairs={{0,1},{1,2},{2,3},{3,4},{4,5},{5,6},{6,7},{8,9},{9,10},{10,11},{11... | collective-permute-start | bytes 393224 | tf_op jit(solution)/shard_map/ppermute | solution.py:16
  61.5 4.6 %collective-permute-start.3 = (bf16[1,256,256]{2,1,0:T(8,128)(2,1)S(1)}, bf16[1,256,256]{2,1,0:T(8,128)(2,1)S(1)}, u32[]{:S(2)}, u32[]{:S(2)}) collective-permute-start(bf16[1,256,256]{2,1,0:T(8,128)(2,1)S(1)} %multiply_convert_fusion), channel_id=1, source_target_pairs={{1,0},{2,1},{3,2},{4,3},{5,4},{6,5},{7,6},{9,8},{10,9},{11,10},{12... | collective-permute-start | bytes 393224 | tf_op jit(solution)/shard_map/ppermute | solution.py:18
  63.0 46.6 %collective-permute-start.5 = (f32[1,64]{1,0:T(1,128)S(1)}, f32[1,64]{1,0:T(1,128)S(1)}, u32[]{:S(2)}, u32[]{:S(2)}) collective-permute-start(f32[1,64]{1,0:T(1,128)S(1)} %slice.15), channel_id=1, source_target_pairs={{0,1},{1,2},{2,3},{3,4},{4,5},{5,6},{6,7},{8,9},{9,10},{10,11},{11... | collective-permute-start | bytes 776 | tf_op jit(solution)/shard_map/ppermute | solution.py:28
  66.2 44.4 %copy-start.3 = (bf16[1,64,512]{2,1,0:T(8,128)(2,1)S(1)}, bf16[1,64,512]{2,1,0:T(8,128)(2,1)}, u32[]{:S(2)}) copy-start(bf16[1,64,512]{2,1,0:T(8,128)(2,1)} %param.21) | copy-start | bytes 196612
  105.8 139.3 %copy-start.1 = (bf16[1,256,256]{2,1,0:T(8,128)(2,1)}, bf16[1,256,256]{2,1,0:T(8,128)(2,1)S(1)}, u32[]{:S(2)}) copy-start(bf16[1,256,256]{2,1,0:T(8,128)(2,1)S(1)} %add_convert_fusion) | copy-start | bytes 393220
  106.1 4.4 %collective-permute-start.4 = (f32[1,64,256]{2,1,0:T(8,128)S(1)}, f32[1,64,256]{2,1,0:T(8,128)S(1)}, u32[]{:S(2)}, u32[]{:S(2)}) collective-permute-start(f32[1,64,256]{2,1,0:T(8,128)S(1)} %slice.17), channel_id=1, source_target_pairs={{0,1},{1,2},{2,3},{3,4},{4,5},{5,6},{6,7},{8,9},{9,10},{10,11},{11... | collective-permute-start | bytes 196616 | tf_op jit(solution)/shard_map/ppermute | solution.py:28
Sparse Core Ops, SparseCore 0:
  111.8 131.4 all-reduce.1
where the time goes:
time: 253 us; the launch traced here: 252 us
  waiting for transfers between devices  135 us (53%)
  matrix products  78.4 us (31%)
  starting transfers between devices  17.2 us (7%)
  between operations  14.3 us (6%)
  other arithmetic  4.43 us (2%)
    psum x1, waiting for transfers between devices, body(): lax.psum(local_grad, ('dp', 'space'))  131 us
    dot_general x54, matrix products, one_tap(): jnp.einsum('wsc,cd->wsd', picked, weight, preferred_element_type=jnp.floa...  76.4 us
    ppermute x2, starting transfers between devices, extended(): lax.ppermute(tail, axis, [(i, (i + 1) % count) for i in range(ends)])  8 us
    ppermute x2, starting transfers between devices, from_behind(): return lax.ppermute(array, axis, pairs)  6.59 us
  transfers between devices with their start and end apart: 7, of which 3 were waited for; matrix products, arithmetic and copies ran while one was open for 16% of the time, Pallas kernels for 0%

commit v1 on v0

--- a/solution.py
+++ b/solution.py
@@ -3,6 +3,12 @@
 import jax.numpy as jnp
 from jax import lax
 from jax.sharding import PartitionSpec as P
+
+
+def add_all(x, axis):
+    pieces = lax.all_gather(x, axis, axis=0, tiled=False)
+    result = pieces.sum(axis=0)
+    return result
 
 
 def extended(cells, sides, width):
@@ -89,7 +95,7 @@
     local_grad = jnp.einsum("wpc,wpd->cd", pooled, cotangent, preferred_element_type=jnp.float32)
     worlds_all = world_rows * lax.axis_size("dp")
     parents_all = par_rows * lax.axis_size("space")
-    down_grad = lax.psum(local_grad, ("dp", "space")) * (1.0 / math.sqrt(worlds_all * parents_all))
+    down_grad = add_all(local_grad, ("dp", "space")) * (1.0 / math.sqrt(worlds_all * parents_all))
     return (fine_out, coarse, down_grad)
 
 

time: 253 us -> 245 us (0.968)
  waiting for transfers between devices: 135 us -> 120 us
  other arithmetic: 4.43 us -> 11.1 us
    psum x1 -> x0, waiting for transfers between devices: 131 us -> none  [body(): lax.psum(local_grad, ('dp', 'space'))]
    all_gather x0 -> x1, waiting for transfers between devices: none -> 116 us  [add_all(): pieces = lax.all_gather(x, axis, axis=0, tiled=False)]
    reduce_sum x0 -> x1, other arithmetic: none -> 7.75 us  [add_all(): result = pieces.sum(axis=0)]
  transfers between devices with their start and end apart: 7 -> 7, of which waited for: 3 -> 3; matrix products, arithmetic and copies ran while one was open for 16% -> 17% of each run, Pallas kernels for 0% -> 0%
where the time goes in v1:
time: 245 us; the launch traced here: 244 us
  waiting for transfers between devices  120 us (49%)
  matrix products  78.4 us (32%)
  starting transfers between devices  17.2 us (7%)
  between operations  14.3 us (6%)
  other arithmetic  11.1 us (5%)
    all_gather x1, waiting for transfers between devices, add_all(): pieces = lax.all_gather(x, axis, axis=0, tiled=False)  116 us
    dot_general x54, matrix products, one_tap(): jnp.einsum('wsc,cd->wsd', picked, weight, preferred_element_type=jnp.floa...  76.4 us
    ppermute x2, starting transfers between devices, extended(): lax.ppermute(tail, axis, [(i, (i + 1) % count) for i in range(ends)])  8 us
    reduce_sum x1, other arithmetic, add_all(): result = pieces.sum(axis=0)  7.75 us
    ppermute x2, starting transfers between devices, from_behind(): return lax.ppermute(array, axis, pairs)  6.59 us
  transfers between devices with their start and end apart: 7, of which 3 were waited for; matrix products, arithmetic and copies ran while one was open for 17% of the time, Pallas kernels for 0%

profile of v1, /device:TPU:0, one launch (start us, length us, event | category | flops | bytes accessed | tf_op | source)
XLA Modules:
  0.0 244.0 jit_solution(2095348619847725217)
XLA Ops:
  7.2 2.5 %collective-permute-start = (bf16[1,256,256]{2,1,0:T(8,128)(2,1)}, bf16[1,256,256]{2,1,0:T(8,128)(2,1)S(1)}, u32[]{:S(2)}, u32[]{:S(2)}) collective-permute-start(bf16[1,256,256]{2,1,0:T(8,128)(2,1)} %param.13), channel_id=1, source_target_pairs={{0,1},{1,2},{2,3},{3,4},{4,5},{5,6},{6,7},{8,9},{9,10},{10,11},{11... | collective-permute-start | bytes 393224 | tf_op jit(solution)/shard_map/ppermute | solution.py:22
  9.8 1.3 collective-permute-start.1
  11.9 3.5 %collective-permute-done.1 = bf16[1,256,256]{2,1,0:T(8,128)(2,1)S(1)} collective-permute-done((bf16[1,256,256]{2,1,0:T(8,128)(2,1)}, bf16[1,256,256]{2,1,0:T(8,128)(2,1)S(1)}, u32[]{:S(2)}, u32[]{:S(2)}) %collective-permute-start.1) | collective-permute-done | bytes 131104 | tf_op jit(solution)/shard_map/ppermute | solution.py:24
  16.4 39.3 %while.22 = (s32[]{:T(128)}, f32[1,256,256]{2,1,0:T(8,128)S(1)}, s32[27,1,256]{2,1,0:T(1,128)S(1)}, bf16[1,768,256]{2,1,0:T(8,128)(2,1)S(1)}, bf16[27,256,256]{2,1,0:T(8,128)(2,1)}, /*index=5*/s32[]{:T(128)}, s32[]{:T(128)}) while((s32[]{:T(128)}, f32[1,256,256]{2,1,0:T(8,128)S(1)}, s32[27,1,256]{2,1,0:T(1,128)S(1)}, ...), condition=%wide.region_1.2_spmd.clone, body=%wide.region_0.1_spmd.clone.sunk | while | flops 134610944 | bytes 1052251 | solution.py:56
  16.4 1.4 fusion.50
  17.8 1.4 fusion.50
  19.3 1.4 fusion.50
  20.8 1.4 fusion.50
  22.2 1.4 fusion.50
  23.7 1.4 fusion.50
  25.1 1.4 fusion.50
  26.6 1.4 fusion.50
  28.0 1.4 fusion.50
  29.5 1.4 fusion.50
  31.0 1.4 fusion.50
  32.4 1.4 fusion.50
  33.9 1.4 fusion.50
  35.3 1.4 fusion.50
  36.8 1.4 fusion.50
  38.2 1.4 fusion.50
  39.7 1.4 fusion.50
  41.2 1.4 fusion.50
  42.6 1.4 fusion.50
  44.1 1.4 fusion.50
  45.5 1.4 fusion.50
  47.0 1.4 fusion.50
  48.4 1.4 fusion.50
  49.9 1.4 fusion.50
  51.3 1.4 fusion.50
  52.8 1.4 fusion.50
  54.3 1.4 fusion.50
  56.0 5.5 %collective-permute-start.2 = (bf16[1,256,256]{2,1,0:T(8,128)(2,1)S(1)}, bf16[1,256,256]{2,1,0:T(8,128)(2,1)S(1)}, u32[]{:S(2)}, u32[]{:S(2)}) collective-permute-start(bf16[1,256,256]{2,1,0:T(8,128)(2,1)S(1)} %multiply_convert_fusion), channel_id=1, source_target_pairs={{0,1},{1,2},{2,3},{3,4},{4,5},{5,6},{6,7},{8,9},{9,10},{10,11},{11... | collective-permute-start | bytes 393224 | tf_op jit(solution)/shard_map/ppermute | solution.py:22
  63.0 3.0 %collective-permute-start.5 = (f32[1,64]{1,0:T(1,128)S(1)}, f32[1,64]{1,0:T(1,128)S(1)}, u32[]{:S(2)}, u32[]{:S(2)}) collective-permute-start(f32[1,64]{1,0:T(1,128)S(1)} %slice.15), channel_id=1, source_target_pairs={{0,1},{1,2},{2,3},{3,4},{4,5},{5,6},{6,7},{8,9},{9,10},{10,11},{11... | collective-permute-start | bytes 776 | tf_op jit(solution)/shard_map/ppermute | solution.py:34
  66.2 39.3 %while.23 = (s32[]{:T(128)}, f32[1,256,256]{2,1,0:T(8,128)S(1)}, s32[27,1,256]{2,1,0:T(1,128)S(1)}, bf16[1,768,256]{2,1,0:T(8,128)(2,1)S(1)}, bf16[27,256,256]{2,1,0:T(8,128)(2,1)}, /*index=5*/s32[]{:T(128)}, s32[]{:T(128)}) while((s32[]{:T(128)}, f32[1,256,256]{2,1,0:T(8,128)S(1)}, s32[27,1,256]{2,1,0:T(1,128)S(1)}, ...), condition=%wide.region_4.5_spmd.clone, body=%wide.region_3.4_spmd.clone.sunk | while | flops 134610944 | bytes 1052251 | solution.py:56
  66.2 1.4 fusion.54
  67.7 1.4 fusion.54
  69.1 1.4 fusion.54
  70.6 1.4 fusion.54
  72.0 1.4 fusion.54
  73.5 1.4 fusion.54
  74.9 1.4 fusion.54
  76.4 1.4 fusion.54
  77.9 1.4 fusion.54
  79.3 1.4 fusion.54
  80.8 1.4 fusion.54
  82.2 1.4 fusion.54
  83.7 1.4 fusion.54
  85.1 1.4 fusion.54
  86.6 1.4 fusion.54
  88.1 1.4 fusion.54
  89.5 1.4 fusion.54
  91.0 1.4 fusion.54
  92.4 1.4 fusion.54
  93.9 1.4 fusion.54
  95.3 1.4 fusion.54
  96.8 1.4 fusion.54
  98.3 1.4 fusion.54
  99.7 1.4 fusion.54
  101.2 1.4 fusion.54
  102.6 1.4 fusion.54
  104.1 1.4 fusion.54
  106.1 3.6 %collective-permute-start.4 = (f32[1,64,256]{2,1,0:T(8,128)S(1)}, f32[1,64,256]{2,1,0:T(8,128)S(1)}, u32[]{:S(2)}, u32[]{:S(2)}) collective-permute-start(f32[1,64,256]{2,1,0:T(8,128)S(1)} %slice.17), channel_id=1, source_target_pairs={{0,1},{1,2},{2,3},{3,4},{4,5},{5,6},{6,7},{8,9},{9,10},{10,11},{11... | collective-permute-start | bytes 196616 | tf_op jit(solution)/shard_map/ppermute | solution.py:34
  112.5 116.1 %all-gather.3.cloned.1.call-done = f32[8192,512]{1,0:T(8,128)} async-done(((f32[256,512]{1,0:T(8,128)}), f32[8192,512]{1,0:T(8,128)}) %all-gather.3.cloned.1.call-update) | async-done | bytes 16777232 | tf_op jit(solution)/shard_map/all_gather | solution.py:9
  228.6 7.8 %reduce_sum.42 = f32[256,512]{1,0:T(8,128)S(1)} reduce(f32[32,256,512]{2,1,0:T(8,128)} %bitcast.75, f32[]{:T(128)} %constant.24.clone.1), dimensions={0}, to_apply=%region_7.8 | reduce | flops 4063232 | bytes 17301508 | tf_op jit(solution)/shard_map/reduce_sum | solution.py:10
  (97 shorter events, 8.2 us)
Async XLA Ops:
  7.2 104.5 %copy-start = (bf16[256,512]{1,0:T(8,128)(2,1)S(1)}, bf16[256,512]{1,0:T(8,128)(2,1)}, u32[]{:S(2)}) copy-start(bf16[256,512]{1,0:T(8,128)(2,1)} %param.20) | copy-start | bytes 786436
  7.2 48.7 %copy-start.5 = (f32[256]{0:T(256)S(1)}, f32[256]{0:T(256)}, u32[]{:S(2)}) copy-start(f32[256]{0:T(256)} %param.18) | copy-start | bytes 3076
  7.2 55.6 %copy-start.4 = (s32[1,256]{1,0:T(1,128)S(1)}, s32[1,256]{1,0:T(1,128)}, u32[]{:S(2)}) copy-start(s32[1,256]{1,0:T(1,128)} %param.15) | copy-start | bytes 3076
  7.2 221.4 %all-gather.3.cloned.1.call-start = ((), (), s32[]{:S(2)}) async-start(), calls=%async_computation | async-start | bytes 17301504 | tf_op jit(solution)/shard_map/all_gather | solution.py:9
  7.2 4.6 %collective-permute-start = (bf16[1,256,256]{2,1,0:T(8,128)(2,1)}, bf16[1,256,256]{2,1,0:T(8,128)(2,1)S(1)}, u32[]{:S(2)}, u32[]{:S(2)}) collective-permute-start(bf16[1,256,256]{2,1,0:T(8,128)(2,1)} %param.13), channel_id=1, source_target_pairs={{0,1},{1,2},{2,3},{3,4},{4,5},{5,6},{6,7},{8,9},{9,10},{10,11},{11... | collective-permute-start | bytes 393224 | tf_op jit(solution)/shard_map/ppermute | solution.py:22
  9.8 5.6 %collective-permute-start.1 = (bf16[1,256,256]{2,1,0:T(8,128)(2,1)}, bf16[1,256,256]{2,1,0:T(8,128)(2,1)S(1)}, u32[]{:S(2)}, u32[]{:S(2)}) collective-permute-start(bf16[1,256,256]{2,1,0:T(8,128)(2,1)} %param.13), channel_id=1, source_target_pairs={{1,0},{2,1},{3,2},{4,3},{5,4},{6,5},{7,6},{9,8},{10,9},{11,10},{12... | collective-permute-start | bytes 393224 | tf_op jit(solution)/shard_map/ppermute | solution.py:24
  55.7 50.0 %copy-start.2 = (bf16[1,256,256]{2,1,0:T(8,128)(2,1)S(1)}, bf16[1,256,256]{2,1,0:T(8,128)(2,1)}, u32[]{:S(2)}) copy-start(bf16[1,256,256]{2,1,0:T(8,128)(2,1)} %param.13) | copy-start | bytes 393220
  55.7 49.9 %copy-start.6 = (f32[256]{0:T(256)S(1)}, f32[256]{0:T(256)}, u32[]{:S(2)}) copy-start(f32[256]{0:T(256)} %param.19) | copy-start | bytes 3076
  56.0 10.1 %collective-permute-start.2 = (bf16[1,256,256]{2,1,0:T(8,128)(2,1)S(1)}, bf16[1,256,256]{2,1,0:T(8,128)(2,1)S(1)}, u32[]{:S(2)}, u32[]{:S(2)}) collective-permute-start(bf16[1,256,256]{2,1,0:T(8,128)(2,1)S(1)} %multiply_convert_fusion), channel_id=1, source_target_pairs={{0,1},{1,2},{2,3},{3,4},{4,5},{5,6},{6,7},{8,9},{9,10},{10,11},{11... | collective-permute-start | bytes 393224 | tf_op jit(solution)/shard_map/ppermute | solution.py:22
  61.5 4.6 %collective-permute-start.3 = (bf16[1,256,256]{2,1,0:T(8,128)(2,1)S(1)}, bf16[1,256,256]{2,1,0:T(8,128)(2,1)S(1)}, u32[]{:S(2)}, u32[]{:S(2)}) collective-permute-start(bf16[1,256,256]{2,1,0:T(8,128)(2,1)S(1)} %multiply_convert_fusion), channel_id=1, source_target_pairs={{1,0},{2,1},{3,2},{4,3},{5,4},{6,5},{7,6},{9,8},{10,9},{11,10},{12... | collective-permute-start | bytes 393224 | tf_op jit(solution)/shard_map/ppermute | solution.py:24
  63.0 46.6 %collective-permute-start.5 = (f32[1,64]{1,0:T(1,128)S(1)}, f32[1,64]{1,0:T(1,128)S(1)}, u32[]{:S(2)}, u32[]{:S(2)}) collective-permute-start(f32[1,64]{1,0:T(1,128)S(1)} %slice.15), channel_id=1, source_target_pairs={{0,1},{1,2},{2,3},{3,4},{4,5},{5,6},{6,7},{8,9},{9,10},{10,11},{11... | collective-permute-start | bytes 776 | tf_op jit(solution)/shard_map/ppermute | solution.py:34
  66.2 44.4 %copy-start.3 = (bf16[1,64,512]{2,1,0:T(8,128)(2,1)S(1)}, bf16[1,64,512]{2,1,0:T(8,128)(2,1)}, u32[]{:S(2)}) copy-start(bf16[1,64,512]{2,1,0:T(8,128)(2,1)} %param.21) | copy-start | bytes 196612
  105.8 130.5 %copy-start.1 = (bf16[1,256,256]{2,1,0:T(8,128)(2,1)}, bf16[1,256,256]{2,1,0:T(8,128)(2,1)S(1)}, u32[]{:S(2)}) copy-start(bf16[1,256,256]{2,1,0:T(8,128)(2,1)S(1)} %add_convert_fusion) | copy-start | bytes 393220
  106.1 4.4 %collective-permute-start.4 = (f32[1,64,256]{2,1,0:T(8,128)S(1)}, f32[1,64,256]{2,1,0:T(8,128)S(1)}, u32[]{:S(2)}, u32[]{:S(2)}) collective-permute-start(f32[1,64,256]{2,1,0:T(8,128)S(1)} %slice.17), channel_id=1, source_target_pairs={{0,1},{1,2},{2,3},{3,4},{4,5},{5,6},{6,7},{8,9},{9,10},{10,11},{11... | collective-permute-start | bytes 196616 | tf_op jit(solution)/shard_map/ppermute | solution.py:34
Sparse Core Ops, SparseCore 0:
  111.8 116.7 all-gather.2
